TPU v7x, 32 devices: a whole 2x2x4 slice. The times are simulated.
32 devices in a mesh: fsdp: 16 (over z, y, core), tp: 2 (over x).
Axes of the slice: x: 2, y: 2, z: 4, core: 2. Of those that a mesh axis runs over, the one named last changes fastest.
Arguments:
- tokens: bfloat16 [16, 1024, 1152], P('fsdp', 'tp'), may hold values from -6 to 6
- condition: bfloat16 [16, 1152], P('fsdp'), may hold values from -3 to 3
- mod_weight: bfloat16 [1152, 6912], P('tp', 'fsdp'), may hold values from -0.088388348 to 0.088388348
- mod_bias: bfloat16 [6912], P('fsdp'), may hold values from -1.5 to 1.5
- qkv_weight: bfloat16 [1152, 3, 1152], P('fsdp', None, 'tp'), may hold values from -0.088388348 to 0.088388348
- qv_bias: bfloat16 [2, 1152], P(None, 'fsdp'), may hold values from -2 to 2
- out_weight: bfloat16 [1152, 1152], P('tp', 'fsdp'), may hold values from -0.75 to 0.75
- out_bias: bfloat16 [1152], P('fsdp'), may hold values from -3 to 3
- up_weight: bfloat16 [1152, 4608], P('fsdp', 'tp'), may hold values from -0.1875 to 0.1875
- up_bias: bfloat16 [4608], P('fsdp'), may hold values from -3 to 3
- down_weight: bfloat16 [4608, 1152], P('tp', 'fsdp'), may hold values from -0.09375 to 0.09375
- down_bias: bfloat16 [1152], P('fsdp'), may hold values from -3 to 3
- cotangent: bfloat16 [16, 1024, 1152], P('fsdp', 'tp'), may hold values from -6 to 6
Outputs:
- result: bfloat16 [16, 1024, 1152], P('fsdp', 'tp')
- tokens_grad: bfloat16 [16, 1024, 1152], P('fsdp', 'tp')
- condition_grad: float32 [16, 1152], P('fsdp', 'tp')
- mod_weight_grad: float32 [1152, 6912], P('tp', 'fsdp')
- mod_bias_grad: float32 [6912], P('fsdp')
- qkv_weight_grad: float32 [1152, 3, 1152], P('fsdp', None, 'tp')
- qv_bias_grad: float32 [2, 1152], P(None, 'fsdp')
- out_weight_grad: float32 [1152, 1152], P('tp', 'fsdp')
- out_bias_grad: float32 [1152], P('fsdp')
- up_weight_grad: float32 [1152, 4608], P('fsdp', 'tp')
- up_bias_grad: float32 [4608], P('fsdp')
- down_weight_grad: float32 [4608, 1152], P('tp', 'fsdp')
- down_bias_grad: float32 [1152], P('fsdp')
All inputs are finite; a program needn't handle non-finite values.
Results may differ from a plain program's by a relative error of at most 0.015.
Values may be sent and summed in bfloat16 or wider, within the bound.
A program may use at most 256 MiB of HBM per device.

v0:
```python
import math
import jax
import jax.numpy as jnp
from jax import lax
from jax.sharding import PartitionSpec as P

HEAD_DIM = 72
EPSILON = 1e-06
HIGH = lax.Precision.HIGHEST


def normalize(values):
    center = values - jnp.mean(values, axis=-1, keepdims=True)
    variance = jnp.mean(center * center, axis=-1, keepdims=True)
    inverse = lax.rsqrt(variance + EPSILON)
    return (center * inverse, inverse)


def norm_back(grad_norm, normed, inverse):
    first_mean = jnp.mean(grad_norm, axis=-1, keepdims=True)
    second_mean = jnp.mean(grad_norm * normed, axis=-1, keepdims=True)
    return inverse * (grad_norm - first_mean - normed * second_mean)


def inner_rows(left, right):
    return lax.dot_general(
        left, right, (((0,), (0,)), ((), ())), preferred_element_type=jnp.float32
    )


def outer_cols(left, right):
    return lax.dot_general(
        left, right, (((1,), (1,)), ((), ())), preferred_element_type=jnp.float32
    )


def gelu_tanh(values):
    return jax.nn.gelu(values, approximate=True)


def to_heads(flat, head_count):
    return flat.reshape(flat.shape[0], head_count, HEAD_DIM).transpose(1, 0, 2)


def from_heads(stacked):
    return stacked.transpose(1, 0, 2).reshape(stacked.shape[1], stacked.shape[0] * HEAD_DIM)


def shards(
    tokens,
    condition,
    mod_weight,
    mod_bias,
    qkv_weight,
    qv_bias,
    out_weight,
    out_bias,
    up_weight,
    up_bias,
    down_weight,
    down_bias,
    cotangent,
):
    tp_count = lax.axis_size("tp")
    tp_place = lax.axis_index("tp")
    local_rows = tokens.shape[1]
    width = tokens.shape[2]
    seq_len = local_rows * tp_count
    share = width // tp_count
    (
        mod_full,
        mod_shift,
        qkv_full,
        qv_full,
        out_full,
        out_shift,
        up_full,
        up_shift,
        down_full,
        down_shift,
    ) = (
        lax.all_gather(mod_weight, "fsdp", axis=1, tiled=True),
        lax.all_gather(mod_bias, "fsdp", axis=0, tiled=True),
        lax.all_gather(qkv_weight, "fsdp", axis=0, tiled=True),
        lax.all_gather(qv_bias, "fsdp", axis=1, tiled=True),
        lax.all_gather(out_weight, "fsdp", axis=1, tiled=True),
        lax.all_gather(out_bias, "fsdp", axis=0, tiled=True),
        lax.all_gather(up_weight, "fsdp", axis=0, tiled=True),
        lax.all_gather(up_bias, "fsdp", axis=0, tiled=True),
        lax.all_gather(down_weight, "fsdp", axis=1, tiled=True),
        lax.all_gather(down_bias, "fsdp", axis=0, tiled=True),
    )
    head_cols = qkv_full.shape[2]
    head_count = head_cols // HEAD_DIM
    hidden_cols = up_full.shape[1]
    cond_row = condition[0].astype(jnp.float32)
    cond_part = lax.dynamic_slice_in_dim(cond_row, tp_place * share, share)
    silu_part, silu_pull = jax.vjp(jax.nn.silu, cond_part)
    silu_low = silu_part.astype(jnp.bfloat16)
    partial_mod = jnp.dot(silu_low[None, :], mod_full, preferred_element_type=jnp.float32)[0]
    modulation = lax.psum(partial_mod, "tp") + mod_shift.astype(jnp.float32)
    pieces = modulation.reshape(6, width)
    shift_one = pieces[0]
    scale_one = pieces[1]
    gate_one = pieces[2]
    shift_two = pieces[3]
    scale_two = pieces[4]
    gate_two = pieces[5]
    rows_in = tokens[0].astype(jnp.float32)
    normed_one, inverse_one = normalize(rows_in)
    hidden_one = lax.all_gather(
        (normed_one * (1.0 + scale_one) + shift_one).astype(jnp.bfloat16), "tp", axis=0, tiled=True
    )
    qkv_matrix = qkv_full.reshape(width, 3 * head_cols)
    projected = jnp.dot(hidden_one, qkv_matrix, preferred_element_type=jnp.float32).reshape(
        seq_len, 3, head_cols
    )
    qv_local = lax.dynamic_slice_in_dim(
        qv_full.astype(jnp.float32), tp_place * head_cols, head_cols, 1
    )
    queries = to_heads((projected[:, 0] + qv_local[0]).astype(jnp.bfloat16), head_count)
    keys_all = to_heads(projected[:, 1].astype(jnp.bfloat16), head_count)
    values_all = to_heads((projected[:, 2] + qv_local[1]).astype(jnp.bfloat16), head_count)
    block = min(512, seq_len)
    block_count = seq_len // block
    scaling = 1.0 / math.sqrt(HEAD_DIM)
    query_blocks = queries.reshape(head_count, block_count, block, HEAD_DIM).transpose(1, 0, 2, 3)

    def attend(query_block):
        scores = (
            jnp.einsum("hqd,hkd->hqk", query_block, keys_all, preferred_element_type=jnp.float32)
            * scaling
        )
        highest = jnp.max(scores, axis=-1, keepdims=True)
        raised = jnp.exp(scores - highest)
        totals = jnp.sum(raised, axis=-1, keepdims=True)
        weights = (raised / totals).astype(jnp.bfloat16)
        output = jnp.einsum("hqk,hkd->hqd", weights, values_all, preferred_element_type=jnp.float32)
        return (output, (highest + jnp.log(totals))[..., 0])

    attended_blocks, log_totals = lax.map(attend, query_blocks)
    attended = attended_blocks.transpose(1, 0, 2, 3).reshape(head_count, seq_len, HEAD_DIM)
    attended_low = from_heads(attended).astype(jnp.bfloat16)
    picked = attended_low
    branch_one = lax.psum_scatter(
        jnp.dot(picked, out_full, preferred_element_type=jnp.float32),
        "tp",
        scatter_dimension=0,
        tiled=True,
    ) + out_shift.astype(jnp.float32)
    middle = rows_in + gate_one * branch_one
    normed_two, inverse_two = normalize(middle)
    hidden_two = lax.all_gather(
        (normed_two * (1.0 + scale_two) + shift_two).astype(jnp.bfloat16), "tp", axis=0, tiled=True
    )
    up_local = lax.dynamic_slice_in_dim(
        up_shift.astype(jnp.float32), tp_place * hidden_cols, hidden_cols
    )
    before = jnp.dot(hidden_two, up_full, preferred_element_type=jnp.float32) + up_local
    activated, gelu_pull = jax.vjp(gelu_tanh, before)
    activated_low = activated.astype(jnp.bfloat16)
    picked = activated_low
    branch_two = lax.psum_scatter(
        jnp.dot(picked, down_full, preferred_element_type=jnp.float32).astype(jnp.bfloat16),
        "tp",
        scatter_dimension=0,
        tiled=True,
    ).astype(jnp.float32) + down_shift.astype(jnp.float32)
    outcome = (middle + gate_two * branch_two).astype(jnp.bfloat16)
    grad_rows = cotangent[0].astype(jnp.float32)
    grad_gate_two = jnp.sum(grad_rows * branch_two, axis=0)
    grad_branch_two = lax.all_gather(
        (grad_rows * gate_two).astype(jnp.bfloat16), "tp", axis=0, tiled=True
    )
    down_bias_term = jnp.sum(grad_branch_two.astype(jnp.float32), axis=0)
    down_weight_term = inner_rows(activated_low, grad_branch_two)
    grad_before = gelu_pull(outer_cols(grad_branch_two, down_full))[0].astype(jnp.bfloat16)
    up_bias_part = jnp.sum(grad_before.astype(jnp.float32), axis=0)
    up_weight_term = inner_rows(hidden_two, grad_before)
    picked = grad_before
    grad_hidden_two = lax.psum_scatter(
        outer_cols(picked, up_full), "tp", scatter_dimension=0, tiled=True
    )
    grad_scale_two = jnp.sum(grad_hidden_two * normed_two, axis=0)
    grad_shift_two = jnp.sum(grad_hidden_two, axis=0)
    grad_middle = grad_rows + norm_back(
        grad_hidden_two * (1.0 + scale_two), normed_two, inverse_two
    )
    grad_gate_one = jnp.sum(grad_middle * branch_one, axis=0)
    grad_branch_one = lax.all_gather(
        (grad_middle * gate_one).astype(jnp.bfloat16), "tp", axis=0, tiled=True
    )
    out_bias_term = jnp.sum(grad_branch_one.astype(jnp.float32), axis=0)
    out_weight_term = inner_rows(attended_low, grad_branch_one)
    grad_attended = outer_cols(grad_branch_one, out_full).astype(jnp.bfloat16)
    grad_blocks = (
        to_heads(grad_attended, head_count)
        .reshape(head_count, block_count, block, HEAD_DIM)
        .transpose(1, 0, 2, 3)
    )

    def attend_back(carry, inputs):
        grad_keys, grad_values = carry
        query_block, log_block, grad_block = inputs
        scores = (
            jnp.einsum("hqd,hkd->hqk", query_block, keys_all, preferred_element_type=jnp.float32)
            * scaling
        )
        weights = jnp.exp(scores - log_block[..., None])
        grad_weights = jnp.einsum(
            "hqd,hkd->hqk", grad_block, values_all, preferred_element_type=jnp.float32
        )
        centered = jnp.sum(weights * grad_weights, axis=-1, keepdims=True)
        grad_scores = (weights * (grad_weights - centered)).astype(jnp.bfloat16)
        grad_query = (
            jnp.einsum("hqk,hkd->hqd", grad_scores, keys_all, preferred_element_type=jnp.float32)
            * scaling
        )
        grad_keys = (
            grad_keys
            + jnp.einsum(
                "hqk,hqd->hkd", grad_scores, query_block, preferred_element_type=jnp.float32
            )
            * scaling
        )
        grad_values = grad_values + jnp.einsum(
            "hqk,hqd->hkd",
            weights.astype(jnp.bfloat16),
            grad_block,
            preferred_element_type=jnp.float32,
        )
        return ((grad_keys, grad_values), grad_query)

    zero_heads = jnp.zeros((head_count, seq_len, HEAD_DIM), jnp.float32)
    (grad_keys, grad_values), grad_query_blocks = lax.scan(
        attend_back, (zero_heads, zero_heads), (query_blocks, log_totals, grad_blocks)
    )
    grad_queries = grad_query_blocks.transpose(1, 0, 2, 3).reshape(head_count, seq_len, HEAD_DIM)
    grad_projected = jnp.stack(
        [from_heads(grad_queries), from_heads(grad_keys), from_heads(grad_values)], axis=1
    ).astype(jnp.bfloat16)
    qv_bias_part = jnp.sum(grad_projected[:, 0::2].astype(jnp.float32), axis=0)
    grad_flat = grad_projected.reshape(seq_len, 3 * head_cols)
    qkv_weight_term = inner_rows(hidden_one, grad_flat).reshape(width, 3, head_cols)
    picked = grad_flat
    grad_hidden_one = lax.psum_scatter(
        outer_cols(picked, qkv_matrix).astype(jnp.bfloat16), "tp", scatter_dimension=0, tiled=True
    ).astype(jnp.float32)
    grad_scale_one = jnp.sum(grad_hidden_one * normed_one, axis=0)
    grad_shift_one = jnp.sum(grad_hidden_one, axis=0)
    grad_tokens = grad_middle + norm_back(
        grad_hidden_one * (1.0 + scale_one), normed_one, inverse_one
    )
    grad_mod_part = jnp.concatenate(
        [
            grad_shift_one,
            grad_scale_one,
            grad_gate_one,
            grad_shift_two,
            grad_scale_two,
            grad_gate_two,
        ]
    )
    qv_padded = lax.dynamic_update_slice_in_dim(
        jnp.zeros((2, width), jnp.float32), qv_bias_part, tp_place * head_cols, 1
    )
    up_padded = lax.dynamic_update_slice_in_dim(
        jnp.zeros((up_shift.shape[0],), jnp.float32), up_bias_part, tp_place * hidden_cols, 0
    )
    grad_mod, qv_bias_term, up_bias_term = (
        lax.psum(grad_mod_part.astype(jnp.bfloat16), "tp").astype(jnp.float32),
        lax.psum(qv_padded.astype(jnp.bfloat16), "tp").astype(jnp.float32),
        lax.psum(up_padded.astype(jnp.bfloat16), "tp").astype(jnp.float32),
    )
    grad_silu = jnp.dot(mod_full.astype(jnp.float32), grad_mod, precision=HIGH)
    cond_grad = silu_pull(grad_silu)[0][None, :]
    mod_weight_term = silu_low.astype(jnp.float32)[:, None] * grad_mod[None, :]
    (
        mod_weight_grad,
        mod_bias_grad,
        qkv_weight_grad,
        qv_bias_grad,
        out_weight_grad,
        out_bias_grad,
        up_weight_grad,
        up_bias_grad,
        down_weight_grad,
        down_bias_grad,
    ) = (
        lax.psum_scatter(mod_weight_term, "fsdp", scatter_dimension=1, tiled=True),
        lax.psum_scatter(grad_mod, "fsdp", scatter_dimension=0, tiled=True),
        lax.psum_scatter(qkv_weight_term, "fsdp", scatter_dimension=0, tiled=True),
        lax.psum_scatter(qv_bias_term, "fsdp", scatter_dimension=1, tiled=True),
        lax.psum_scatter(out_weight_term, "fsdp", scatter_dimension=1, tiled=True),
        lax.psum_scatter(out_bias_term, "fsdp", scatter_dimension=0, tiled=True),
        lax.psum_scatter(up_weight_term, "fsdp", scatter_dimension=0, tiled=True),
        lax.psum_scatter(up_bias_term, "fsdp", scatter_dimension=0, tiled=True),
        lax.psum_scatter(down_weight_term, "fsdp", scatter_dimension=1, tiled=True),
        lax.psum_scatter(down_bias_term, "fsdp", scatter_dimension=0, tiled=True),
    )
    return (
        outcome[None],
        grad_tokens.astype(jnp.bfloat16)[None],
        cond_grad,
        mod_weight_grad,
        mod_bias_grad,
        qkv_weight_grad,
        qv_bias_grad,
        out_weight_grad,
        out_bias_grad,
        up_weight_grad,
        up_bias_grad,
        down_weight_grad,
        down_bias_grad,
    )


def solution(mesh):
    return jax.shard_map(
        shards,
        mesh=mesh,
        in_specs=(
            P("fsdp", "tp", None),
            P("fsdp", None),
            P("tp", "fsdp"),
            P("fsdp"),
            P("fsdp", None, "tp"),
            P(None, "fsdp"),
            P("tp", "fsdp"),
            P("fsdp"),
            P("fsdp", "tp"),
            P("fsdp"),
            P("tp", "fsdp"),
            P("fsdp"),
            P("fsdp", "tp", None),
        ),
        out_specs=(
            P("fsdp", "tp", None),
            P("fsdp", "tp", None),
            P("fsdp", "tp"),
            P("tp", "fsdp"),
            P("fsdp"),
            P("fsdp", None, "tp"),
            P(None, "fsdp"),
            P("tp", "fsdp"),
            P("fsdp"),
            P("fsdp", "tp"),
            P("fsdp"),
            P("tp", "fsdp"),
            P("fsdp"),
        ),
        check_vma=False,
    )
```

profile of v0, /device:TPU:0, one launch (start us, length us, event | category | flops | bytes accessed | tf_op | source)
XLA Modules:
  0.0 1452.1 jit_solution(4694295346993704896)
XLA Ops:
  17.4 65.6 %all-reduce.11 = (bf16[6912]{0:T(1024)(128)(2,1)S(1)}, bf16[1152]{0:T(1024)(128)(2,1)}, bf16[4608]{0:T(1024)(128)(2,1)}, bf16[1152]{0:T(1024)(128)(2,1)}) all-reduce(bf16[6912]{0:T(1024)(128)(2,1)S(1)} %dynamic-update-slice, bf16[1152]{0:T(1024)(128)(2,1)S(1)} %dynamic-update-slice.1, ...), channel_id=1, replica_groups=mesh['fsdp'=16,'tp'=2] {'fsdp'}, use_global_device_ids=true, to_apply=%add | all-reduce | flops 13824 | bytes 55296
  109.2 18.8 %all-gather = bf16[16,72,2]{1,2,0:T(2,128)(2,1)S(1)} all-gather(bf16[1,72,2]{1,2,0:T(2,128)(2,1)S(1)} %bitcast.228), channel_id=1, replica_groups=mesh['fsdp'=16,'tp'=2] {'fsdp'}, dimensions={0}, use_global_device_ids=true | all-gather | bytes 4896 | tf_op jit(solution)/shard_map/all_gather | solution.py:85
  128.4 15.3 %all-gather.15.cloned.1.call-done = bf16[1152,3,576]{2,0,1:T(8,128)(2,1)} async-done(((bf16[72,3,576]{2,0,1:T(8,128)(2,1)}), bf16[1152,3,576]{2,0,1:T(8,128)(2,1)}) %all-gather.15.cloned.1.call-update) | async-done | bytes 3981328 | tf_op jit(solution)/shard_map/all_gather | solution.py:84
  150.2 30.2 %all-gather.13.cloned.1.call-done = bf16[1024,1152]{1,0:T(8,128)(2,1)} async-done(((bf16[512,1152]{1,0:T(8,128)(2,1)}), bf16[1024,1152]{1,0:T(8,128)(2,1)}) %all-gather.13.cloned.1.call-update) | async-done | bytes 2359312 | tf_op jit(solution)/shard_map/all_gather | solution.py:111
  194.1 24.2 %while.27 = (s32[]{:T(128)}, bf16[2,8,512,72]{2,3,1,0:T(8,128)(2,1)}, f32[2,8,512]{2,1,0:T(8,128)}, bf16[2,8,512,72]{2,3,1,0:T(8,128)(2,1)S(1)}, bf16[8,1024,72]...) while((s32[]{:T(128)}, bf16[2,8,512,72]{2,3,1,0:T(8,128)(2,1)}, ...), condition=%wide.region_6.7_spmd, body=%wide.region_3.6_spmd.sunk | while | flops 1245704192 | bytes 64291024 | solution.py:141
  229.3 57.8 %reduce-scatter.13.cloned.1.call-done = f32[512,1152]{1,0:T(8,128)} async-done(((f32[1024,1152]{1,0:T(8,128)}), f32[512,1152]{1,0:T(8,128)}) %reduce-scatter.13.cloned.1.call-update) | async-done | bytes 2359312 | tf_op jit(solution)/shard_map/reduce_scatter | solution.py:145
  297.4 48.3 %all-gather.21.cloned.1.call-done = bf16[1152,2304]{1,0:T(8,128)(2,1)} async-done(((bf16[72,2304]{1,0:T(8,128)(2,1)}), bf16[1152,2304]{1,0:T(8,128)(2,1)}) %all-gather.21.cloned.1.call-update) | async-done | bytes 5308432 | tf_op jit(solution)/shard_map/all_gather | solution.py:88
  345.7 36.9 %all-gather.19.cloned.1.call-done = bf16[1024,1152]{1,0:T(8,128)(2,1)} async-done(((bf16[512,1152]{1,0:T(8,128)(2,1)}), bf16[1024,1152]{1,0:T(8,128)(2,1)}) %all-gather.19.cloned.1.call-update) | async-done | bytes 2359312 | tf_op jit(solution)/shard_map/all_gather | solution.py:153
  382.6 11.4 fusion.82
  394.0 47.4 %all-gather.23.cloned.1.call-done = bf16[2304,1152]{0,1:T(8,128)(2,1)} async-done(((bf16[2304,72]{0,1:T(8,128)(2,1)}), bf16[2304,1152]{0,1:T(8,128)(2,1)}) %all-gather.23.cloned.1.call-update) | async-done | bytes 5308432 | tf_op jit(solution)/shard_map/all_gather | solution.py:90
  441.4 36.9 %all-gather.25.cloned.1.call-done = bf16[1024,1152]{1,0:T(8,128)(2,1)} async-done(((bf16[512,1152]{1,0:T(8,128)(2,1)}), bf16[1024,1152]{1,0:T(8,128)(2,1)}) %all-gather.25.cloned.1.call-update) | async-done | bytes 2359312 | tf_op jit(solution)/shard_map/all_gather | solution.py:172
  478.2 15.4 %convert_reduce_fusion = (bf16[2304]{0:T(1024)(128)(2,1)}, bf16[1024,2304]{1,0:T(8,128)(2,1)S(1)}) fusion(f32[1024,2304]{1,0:T(8,128)} %fusion.82, f32[2304]{0:T(1024)} %dynamic-slice_convert_fusion, bf16[1024,1152]{1,0:T(8,128)(2,1)} %all-gather.25.cloned.1.call-done, bf16[2304,1152]{0,1:T(8,128)(2,1)} %all-gather.23.cloned.1.call-done), kind=kOutput, calls=%fused_computation.50 | convolution fusion | flops 5490079744 | bytes 21837312 | tf_op jit(solution)/shard_map/dot_general | solution.py:32
  495.7 10.4 fusion.83
  506.6 13.4 convolution_convert_fusion
  521.4 44.8 %reduce-scatter.17.cloned.1.call-done = f32[512,1152]{1,0:T(8,128)} async-done(((f32[1024,1152]{1,0:T(8,128)}), f32[512,1152]{1,0:T(8,128)}) %reduce-scatter.17.cloned.1.call-update) | async-done | bytes 2359312 | tf_op jit(solution)/shard_map/reduce_scatter | solution.py:181
  570.8 32.5 %reduce-scatter.15.cloned.1.call-done = bf16[512,1152]{1,0:T(8,128)(2,1)} async-done(((bf16[1024,1152]{1,0:T(8,128)(2,1)}), bf16[512,1152]{1,0:T(8,128)(2,1)}) %reduce-scatter.15.cloned.1.call-update) | async-done | bytes 1179664 | tf_op jit(solution)/shard_map/reduce_scatter | solution.py:163
  612.1 36.2 %all-gather.27.cloned.1.call-done = bf16[1024,1152]{1,0:T(8,128)(2,1)} async-done(((bf16[512,1152]{1,0:T(8,128)(2,1)}), bf16[1024,1152]{1,0:T(8,128)(2,1)}) %all-gather.27.cloned.1.call-update) | async-done | bytes 2359312 | tf_op jit(solution)/shard_map/all_gather | solution.py:190
  660.7 116.9 %while.28 = (s32[]{:T(128)}, f32[8,1024,72]{1,2,0:T(8,128)}, f32[8,1024,72]{1,2,0:T(8,128)}, bf16[2,8,512,72]{2,3,1,0:T(8,128)(2,1)}, bf16[2,8,512,72]{2,3,1,0:T...) while((s32[]{:T(128)}, f32[8,1024,72]{1,2,0:T(8,128)}, ...), condition=%wide.region_16.17_spmd.clone, body=%wide.region_14.16_spmd.clone.sunk | while | flops 3073470464 | bytes 271434112 | solution.py:235
  669.8 10.3 select_add_fusion.5
  680.1 14.5 multiply_reduce_fusion.10
  697.0 10.5 multiply_convert_fusion.8
  726.9 11.1 select_add_fusion.5
  738.0 14.5 multiply_reduce_fusion.10
  754.8 10.5 multiply_convert_fusion.8
  795.8 12.4 fusion.73
  808.3 11.5 fusion.85
  820.1 9.5 fusion.42
  864.9 61.7 %all-reduce.10 = (f32[6912]{0:T(1024)}, f32[2,1152]{1,0:T(2,128)}, f32[1152]{0:T(1024)}, f32[4608]{0:T(1024)}, f32[1152]{0:T(1024)}) all-reduce(bf16[6912]{0:T(1024)(128)(2,1)} %copy-done.25, bf16[2,1152]{1,0:T(2,128)(2,1)} %get-tuple-element.224, f32[1152]{0:T(1024)} %convert_reduce_fusion.2, ...), channel_id=7, replica_groups=mesh['fsdp'=16,'tp'=2] {'fsdp'}, use_global_device_ids=true, to_apply=%region_28.29.clone | all-reduce | flops 16128 | bytes 101376
  937.6 80.0 %reduce-scatter.27.cloned.1.call-done = f32[2304,72]{0,1:T(8,128)} async-done(((f32[2304,1152]{0,1:T(8,128)}), f32[2304,72]{0,1:T(8,128)}) %reduce-scatter.27.cloned.1.call-update) | async-done | bytes 663568 | tf_op jit(solution)/shard_map/reduce_scatter | solution.py:298
  1017.6 124.5 %reduce-scatter.25.cloned.1.call-done = f32[72,2304]{1,0:T(8,128)} async-done(((f32[1152,2304]{1,0:T(8,128)}), f32[72,2304]{1,0:T(8,128)}) %reduce-scatter.25.cloned.1.call-update) | async-done | bytes 663568 | tf_op jit(solution)/shard_map/reduce_scatter | solution.py:296
  1142.1 111.3 %reduce-scatter.23.cloned.1.call-done = f32[72,3,576]{2,0,1:T(8,128)} async-done(((f32[1152,3,576]{2,0,1:T(8,128)}), f32[72,3,576]{2,0,1:T(8,128)}) %reduce-scatter.23.cloned.1.call-update) | async-done | bytes 497680 | tf_op jit(solution)/shard_map/reduce_scatter | solution.py:292
  1253.5 191.4 %reduce-scatter.21.cloned.1.call-done = f32[576,432]{0,1:T(8,128)} async-done(((f32[576,6912]{0,1:T(8,128)}), f32[576,432]{0,1:T(8,128)}) %reduce-scatter.21.cloned.1.call-update) | async-done | bytes 995344 | tf_op jit(solution)/shard_map/reduce_scatter | solution.py:290
  (272 shorter events, 237.6 us)
Async XLA Ops:
  7.2 77.3 %copy-start.10 = (bf16[1,512,1152]{2,1,0:T(8,128)(2,1)S(1)}, bf16[1,512,1152]{2,1,0:T(8,128)(2,1)}, u32[]{:S(2)}) copy-start(bf16[1,512,1152]{2,1,0:T(8,128)(2,1)} %param.17) | copy-start | bytes 3538948
  7.2 84.4 %all-gather.11.cloned.1.call-start = ((), (), s32[]{:S(2)}) async-start(), calls=%async_computation.9 | async-start | bytes 9400320 | tf_op jit(solution)/shard_map/all_gather | solution.py:82
  7.9 135.8 %all-gather.15.cloned.1.call-start = ((), (), s32[]{:S(2)}) async-start(), calls=%async_computation.11 | async-start | bytes 4700160 | tf_op jit(solution)/shard_map/all_gather | solution.py:84
  8.7 171.8 %all-gather.13.cloned.1.call-start = ((), (), s32[]{:S(2)}) async-start(), calls=%async_computation.10 | async-start | bytes 3538944 | tf_op jit(solution)/shard_map/all_gather | solution.py:111
  84.5 21.9 %copy-start.29 = (f32[512]{0:T(512)}, f32[512]{0:T(512)S(1)}, u32[]{:S(2)}) copy-start(f32[512]{0:T(512)S(1)} %broadcast_multiply_fusion.6) | copy-start | bytes 6148
  85.0 21.5 %copy-start.34 = (f32[512]{0:T(512)}, f32[512]{0:T(512)S(1)}, u32[]{:S(2)}) copy-start(f32[512]{0:T(512)S(1)} %add_rsqrt_fusion.1) | copy-start | bytes 6148
  97.5 11.7 copy-start.45
  108.6 113.2 %all-gather.17.cloned.1.call-start = ((), (), s32[]{:S(2)}) async-start(), calls=%async_computation.12 | async-start | bytes 1566720 | tf_op jit(solution)/shard_map/all_gather | solution.py:86
  109.2 177.9 %reduce-scatter.13.cloned.1.call-start = ((), (), s32[]{:S(2)}) async-start(), calls=%async_computation.13 | async-start | bytes 7077888 | tf_op jit(solution)/shard_map/reduce_scatter | solution.py:145
  227.9 59.2 %copy-start.27 = (f32[1152]{0:T(1024)S(1)}, f32[1152]{0:T(1024)}, u32[]{:S(2)}) copy-start(f32[1152]{0:T(1024)} %get-tuple-element.247) | copy-start | bytes 13828
  227.9 117.8 %all-gather.21.cloned.1.call-start = ((), (), s32[]{:S(2)}) async-start(), calls=%async_computation.15 | async-start | bytes 5640192 | tf_op jit(solution)/shard_map/all_gather | solution.py:88
  228.5 154.1 %all-gather.19.cloned.1.call-start = ((), (), s32[]{:S(2)}) async-start(), calls=%async_computation.14 | async-start | bytes 3538944 | tf_op jit(solution)/shard_map/all_gather | solution.py:153
  229.3 57.8 %copy-start.28 = (f32[1152]{0:T(1024)}, f32[1152]{0:T(1024)S(1)}, u32[]{:S(2)}) copy-start(f32[1152]{0:T(1024)S(1)} %convert_element_type.164) | copy-start | bytes 13828
  292.5 148.9 %all-gather.23.cloned.1.call-start = ((), (), s32[]{:S(2)}) async-start(), calls=%async_computation.16 | async-start | bytes 5640192 | tf_op jit(solution)/shard_map/all_gather | solution.py:90
  293.2 185.0 %all-gather.25.cloned.1.call-start = ((), (), s32[]{:S(2)}) async-start(), calls=%async_computation.18 | async-start | bytes 3538944 | tf_op jit(solution)/shard_map/all_gather | solution.py:172
  295.8 270.5 %reduce-scatter.17.cloned.1.call-start = ((), (), s32[]{:S(2)}) async-start(), calls=%async_computation.19 | async-start | bytes 7077888 | tf_op jit(solution)/shard_map/reduce_scatter | solution.py:181
  506.1 97.2 %reduce-scatter.15.cloned.1.call-start = ((), (), s32[]{:S(2)}) async-start(), calls=%async_computation.17 | async-start | bytes 3538944 | tf_op jit(solution)/shard_map/reduce_scatter | solution.py:163
  520.1 128.1 %all-gather.27.cloned.1.call-start = ((), (), s32[]{:S(2)}) async-start(), calls=%async_computation.20 | async-start | bytes 3538944 | tf_op jit(solution)/shard_map/all_gather | solution.py:190
  612.0 220.7 %reduce-scatter.19.cloned.1.call-start = ((), (), s32[]{:S(2)}) async-start(), calls=%async_computation.21 | async-start | bytes 3538944 | tf_op jit(solution)/shard_map/reduce_scatter | solution.py:246
  660.8 8.9 copy-start.2
  680.1 16.9 %copy-start = (f32[8,512,1024]{2,1,0:T(8,128)S(1)}, f32[8,512,1024]{2,1,0:T(8,128)}, u32[]{:S(2)}) copy-start(f32[8,512,1024]{2,1,0:T(8,128)} %fusion.143) | copy-start | bytes 50331652 | tf_op jit(solution)/shard_map/while
  717.9 8.9 copy-start.2
  717.9 8.9 copy-start.4
  738.0 16.9 %copy-start = (f32[8,512,1024]{2,1,0:T(8,128)S(1)}, f32[8,512,1024]{2,1,0:T(8,128)}, u32[]{:S(2)}) copy-start(f32[8,512,1024]{2,1,0:T(8,128)} %fusion.143) | copy-start | bytes 50331652 | tf_op jit(solution)/shard_map/while
  782.1 38.0 %copy-start.14 = (bf16[1024,3,576]{0,2,1:T(8,128)(2,1)}, bf16[1024,3,576]{0,2,1:T(8,128)(2,1)S(1)}, u32[]{:S(2)}) copy-start(bf16[1024,3,576]{0,2,1:T(8,128)(2,1)S(1)} %maximum_convert_fusion) | copy-start | bytes 10616836
  789.3 148.3 %reduce-scatter.29.cloned.1.call-start = ((), (), s32[]{:S(2)}) async-start(), calls=%async_computation.26 | async-start | bytes 3133440
  795.1 222.5 %reduce-scatter.27.cloned.1.call-start = ((), (), s32[]{:S(2)}) async-start(), calls=%async_computation.25 | async-start | bytes 11280384 | tf_op jit(solution)/shard_map/reduce_scatter | solution.py:298
  808.2 333.9 %reduce-scatter.25.cloned.1.call-start = ((), (), s32[]{:S(2)}) async-start(), calls=%async_computation.24 | async-start | bytes 11280384 | tf_op jit(solution)/shard_map/reduce_scatter | solution.py:296
  819.8 433.7 %reduce-scatter.23.cloned.1.call-start = ((), (), s32[]{:S(2)}) async-start(), calls=%async_computation.23 | async-start | bytes 9400320 | tf_op jit(solution)/shard_map/reduce_scatter | solution.py:292
  829.6 615.2 %reduce-scatter.21.cloned.1.call-start = ((), (), s32[]{:S(2)}) async-start(), calls=%async_computation.22 | async-start | bytes 18800640 | tf_op jit(solution)/shard_map/reduce_scatter | solution.py:290
  832.5 14.7 %copy-start.42 = (f32[576]{0:T(1024)S(1)}, f32[576]{0:T(1024)}, u32[]{:S(2)}) copy-start(f32[576]{0:T(1024)} %get-tuple-element.226) | copy-start | bytes 6916
  859.3 75.1 %copy-start.13 = (f32[512,1152]{1,0:T(8,128)S(1)}, f32[512,1152]{1,0:T(8,128)}, u32[]{:S(2)}) copy-start(f32[512,1152]{1,0:T(8,128)} %copy-done.12) | copy-start | bytes 7077892
  (47 other events, 176.0 us)
Sparse Core Ops, SparseCore 0:
  10.2 81.3 all-gather.10
  93.8 49.8 all-gather.14
  145.8 34.5 all-gather.12
  182.4 39.3 all-gather.16
  228.1 58.9 reduce-scatter.12
  289.3 56.3 all-gather.20
  347.9 34.6 all-gather.18
  385.0 56.3 all-gather.22
  443.6 34.6 all-gather.24
  506.2 59.9 reduce-scatter.16
  568.5 34.7 reduce-scatter.14
  612.1 36.0 all-gather.26
  789.4 34.6 reduce-scatter.18
  828.5 65.4 reduce-scatter.28
  898.5 119.1 reduce-scatter.26
  1022.1 119.9 reduce-scatter.24
  1146.7 106.7 reduce-scatter.22
  1258.7 186.1 reduce-scatter.20
where the time goes:
time: 1460 us; the launch traced here: 1450 us
  waiting for transfers between devices  904 us (62%)
  matrix products  229 us (16%)
  blocking collectives  163 us (11%)
  other arithmetic  78.6 us (5%)
  local copies, waits for them, and re-layouts  56 us (4%)
  between operations  19.3 us (1%)
    reduce_scatter x1, waiting for transfers between devices, shards(): lax.psum_scatter(mod_weight_term, 'fsdp', scatter_dimension=1, tiled=True)  191 us
    unnamed x2, blocking collectives  127 us
    reduce_scatter x1, waiting for transfers between devices, shards(): lax.psum_scatter(up_weight_term, 'fsdp', scatter_dimension=0, tiled=True)  124 us
    reduce_scatter x1, waiting for transfers between devices, shards(): lax.psum_scatter(qkv_weight_term, 'fsdp', scatter_dimension=0, tiled=True)  111 us
    reduce_scatter x1, waiting for transfers between devices, shards(): lax.psum_scatter(down_weight_term, 'fsdp', scatter_dimension=1, tiled=True)  80 us
    reduce_scatter x1, waiting for transfers between devices, shards(): lax.psum_scatter(jnp.dot(picked, out_full, preferred_element_type=jnp.flo...  57.8 us
    all_gather x1, waiting for transfers between devices, shards(): lax.all_gather(up_weight, 'fsdp', axis=0, tiled=True)  48.3 us
    all_gather x1, waiting for transfers between devices, shards(): lax.all_gather(down_weight, 'fsdp', axis=1, tiled=True)  47.4 us
  transfers between devices with their start and end apart: 18, of which 16 were waited for; matrix products, arithmetic and copies ran while one was open for 12% of the time, Pallas kernels for 0%

commit v1 on v0

--- a/solution.py
+++ b/solution.py
@@ -7,6 +7,28 @@
 HEAD_DIM = 72
 EPSILON = 1e-06
 HIGH = lax.Precision.HIGHEST
+
+
+def joined_along(blocks, dim):
+    blocks = jnp.moveaxis(blocks, 0, dim)
+    lengths = blocks.shape
+    return blocks.reshape(*lengths[:dim], lengths[dim] * lengths[dim + 1], *lengths[dim + 2 :])
+
+
+def gather_around(x, axis, dim):
+    size = lax.axis_size(axis)
+    pairs = [(i, (i + 1) % size) for i in range(size)]
+    back = [(b, a) for a, b in pairs]
+    lower, upper = ([], [])
+    for step in range(size - 1):
+        if step % 2 == 0:
+            lower.append(lax.ppermute(lower[-1] if lower else x, axis, pairs))
+        else:
+            upper.append(lax.ppermute(upper[-1] if upper else x, axis, back))
+    blocks = jnp.stack([*lower[::-1], x, *upper])
+    shift = lax.axis_index(axis) - len(lower)
+    blocks = blocks[(jnp.arange(size) - shift) % size]
+    return joined_along(blocks, dim)
 
 
 def normalize(values):
@@ -87,7 +109,7 @@
         lax.all_gather(out_bias, "fsdp", axis=0, tiled=True),
         lax.all_gather(up_weight, "fsdp", axis=0, tiled=True),
         lax.all_gather(up_bias, "fsdp", axis=0, tiled=True),
-        lax.all_gather(down_weight, "fsdp", axis=1, tiled=True),
+        gather_around(down_weight, "fsdp", 1),
         lax.all_gather(down_bias, "fsdp", axis=0, tiled=True),
     )
     head_cols = qkv_full.shape[2]

time: 1460 us -> 1400 us (0.959)
  waiting for transfers between devices: 904 us -> 790 us
  starting transfers between devices: 1.7 us -> 33.9 us
  local copies, waits for them, and re-layouts: 56 us -> 83.7 us
    reduce_scatter x1, waiting for transfers between devices: 57.8 us -> 0.01 us  [shards(): lax.psum_scatter(jnp.dot(picked, out_full, preferred_element_type=jnp.flo...]
    all_gather x1 -> x0, waiting for transfers between devices: 47.4 us -> none  [shards(): lax.all_gather(down_weight, 'fsdp', axis=1, tiled=True)]
    ppermute x0 -> x15, waiting for transfers between devices: none -> 41.9 us  [the longest x8 40.4 us: gather_around(): lower.append(lax.ppermute(lower[-1] if lower else x, axis, pairs))]
    all_gather x1, waiting for transfers between devices: 48.3 us -> 7.82 us  [shards(): lax.all_gather(up_weight, 'fsdp', axis=0, tiled=True)]
    ppermute x0 -> x15, starting transfers between devices: none -> 32.8 us  [the longest x7 32.5 us: gather_around(): upper.append(lax.ppermute(upper[-1] if upper else x, axis, back))]
    unnamed x94 -> x145, local copies, waits for them, and re-layouts: 24.7 us -> 44.7 us
  transfers between devices with their start and end apart: 18 -> 32, of which waited for: 16 -> 24; matrix products, arithmetic and copies ran while one was open for 12% -> 14% of each run, Pallas kernels for 0% -> 0%
where the time goes in v1:
time: 1400 us; the launch traced here: 1390 us
  waiting for transfers between devices  790 us (56%)
  matrix products  227 us (16%)
  blocking collectives  163 us (12%)
  local copies, waits for them, and re-layouts  83.7 us (6%)
  other arithmetic  78.1 us (6%)
  starting transfers between devices  33.9 us (2%)
  between operations  18.9 us (1%)
    reduce_scatter x1, waiting for transfers between devices, shards(): lax.psum_scatter(mod_weight_term, 'fsdp', scatter_dimension=1, tiled=True)  191 us
    unnamed x2, blocking collectives  127 us
    reduce_scatter x1, waiting for transfers between devices, shards(): lax.psum_scatter(up_weight_term, 'fsdp', scatter_dimension=0, tiled=True)  124 us
    reduce_scatter x1, waiting for transfers between devices, shards(): lax.psum_scatter(qkv_weight_term, 'fsdp', scatter_dimension=0, tiled=True)  111 us
    reduce_scatter x1, waiting for transfers between devices, shards(): lax.psum_scatter(down_weight_term, 'fsdp', scatter_dimension=1, tiled=True)  80.3 us
    reduce_scatter x1, waiting for transfers between devices, shards(): lax.psum_scatter(outer_cols(picked, up_full), 'tp', scatter_dimension=0,...  45.1 us
    unnamed x145, local copies, waits for them, and re-layouts  44.7 us
    ppermute x8, waiting for transfers between devices, gather_around(): lower.append(lax.ppermute(lower[-1] if lower else x, axis, pairs))  40.4 us
  transfers between devices with their start and end apart: 32, of which 24 were waited for; matrix products, arithmetic and copies ran while one was open for 14% of the time, Pallas kernels for 0%

profile of v1, /device:TPU:0, one launch (start us, length us, event | category | flops | bytes accessed | tf_op | source)
XLA Modules:
  0.0 1394.8 jit_solution(15779288597856709453)
XLA Ops:
  17.4 65.6 %all-reduce.11 = (bf16[6912]{0:T(1024)(128)(2,1)S(1)}, bf16[1152]{0:T(1024)(128)(2,1)}, bf16[4608]{0:T(1024)(128)(2,1)}, bf16[1152]{0:T(1024)(128)(2,1)}) all-reduce(bf16[6912]{0:T(1024)(128)(2,1)S(1)} %dynamic-update-slice, bf16[1152]{0:T(1024)(128)(2,1)S(1)} %dynamic-update-slice.1, ...), channel_id=1, replica_groups=mesh['fsdp'=16,'tp'=2] {'fsdp'}, use_global_device_ids=true, to_apply=%add | all-reduce | flops 13824 | bytes 55296
  97.5 8.3 psum.28
  109.2 19.0 %all-gather = bf16[16,72,2]{1,2,0:T(2,128)(2,1)S(1)} all-gather(bf16[1,72,2]{1,2,0:T(2,128)(2,1)S(1)} %bitcast.267), channel_id=1, replica_groups=mesh['fsdp'=16,'tp'=2] {'fsdp'}, dimensions={0}, use_global_device_ids=true | all-gather | bytes 4896 | tf_op jit(solution)/shard_map/all_gather | solution.py:107
  128.6 15.1 %all-gather.14.cloned.1.call-done = bf16[1152,3,576]{2,0,1:T(8,128)(2,1)} async-done(((bf16[72,3,576]{2,0,1:T(8,128)(2,1)}), bf16[1152,3,576]{2,0,1:T(8,128)(2,1)}) %all-gather.14.cloned.1.call-update) | async-done | bytes 3981328 | tf_op jit(solution)/shard_map/all_gather | solution.py:106
  150.3 30.2 %all-gather.12.cloned.1.call-done = bf16[1024,1152]{1,0:T(8,128)(2,1)} async-done(((bf16[512,1152]{1,0:T(8,128)(2,1)}), bf16[1024,1152]{1,0:T(8,128)(2,1)}) %all-gather.12.cloned.1.call-update) | async-done | bytes 2359312 | tf_op jit(solution)/shard_map/all_gather | solution.py:133
  194.2 24.2 %while.27 = (s32[]{:T(128)}, bf16[2,8,512,72]{2,3,1,0:T(8,128)(2,1)}, f32[2,8,512]{2,1,0:T(8,128)}, bf16[2,8,512,72]{2,3,1,0:T(8,128)(2,1)S(1)}, bf16[8,1024,72]...) while((s32[]{:T(128)}, bf16[2,8,512,72]{2,3,1,0:T(8,128)(2,1)}, ...), condition=%wide.region_6.7_spmd, body=%wide.region_3.6_spmd.sunk | while | flops 1245704192 | bytes 64291024 | solution.py:163
  228.4 9.2 collective-permute-done
  348.0 36.9 %all-gather.18.cloned.1.call-done = bf16[1024,1152]{1,0:T(8,128)(2,1)} async-done(((bf16[512,1152]{1,0:T(8,128)(2,1)}), bf16[1024,1152]{1,0:T(8,128)(2,1)}) %all-gather.18.cloned.1.call-update) | async-done | bytes 2359312 | tf_op jit(solution)/shard_map/all_gather | solution.py:175
  384.8 11.4 fusion.84
  396.3 26.8 %all-gather.22.cloned.1.call-done = bf16[1024,1152]{1,0:T(8,128)(2,1)} async-done(((bf16[512,1152]{1,0:T(8,128)(2,1)}), bf16[1024,1152]{1,0:T(8,128)(2,1)}) %all-gather.22.cloned.1.call-update) | async-done | bytes 2359312 | tf_op jit(solution)/shard_map/all_gather | solution.py:194
  423.1 15.5 %convert_reduce_fusion = (bf16[2304]{0:T(1024)(128)(2,1)}, bf16[1024,2304]{1,0:T(8,128)(2,1)S(1)}) fusion(f32[1024,2304]{1,0:T(8,128)} %fusion.84, f32[2304]{0:T(1024)} %dynamic-slice_convert_fusion, bf16[1024,1152]{1,0:T(8,128)(2,1)} %all-gather.22.cloned.1.call-done, bf16[2304,1152]{0,1:T(8,128)(2,1)} %bitcast.254), kind=kOutput, calls=%fused_computation.51 | convolution fusion | flops 5490079744 | bytes 21837312 | tf_op jit(solution)/shard_map/dot_general | solution.py:54
  449.0 13.5 convolution_convert_fusion
  463.8 45.1 %reduce-scatter.17.cloned.1.call-done = f32[512,1152]{1,0:T(8,128)} async-done(((f32[1024,1152]{1,0:T(8,128)}), f32[512,1152]{1,0:T(8,128)}) %reduce-scatter.17.cloned.1.call-update) | async-done | bytes 2359312 | tf_op jit(solution)/shard_map/reduce_scatter | solution.py:203
  513.4 32.3 %reduce-scatter.15.cloned.1.call-done = bf16[512,1152]{1,0:T(8,128)(2,1)} async-done(((bf16[1024,1152]{1,0:T(8,128)(2,1)}), bf16[512,1152]{1,0:T(8,128)(2,1)}) %reduce-scatter.15.cloned.1.call-update) | async-done | bytes 1179664 | tf_op jit(solution)/shard_map/reduce_scatter | solution.py:185
  554.5 36.2 %all-gather.24.cloned.1.call-done = bf16[1024,1152]{1,0:T(8,128)(2,1)} async-done(((bf16[512,1152]{1,0:T(8,128)(2,1)}), bf16[1024,1152]{1,0:T(8,128)(2,1)}) %all-gather.24.cloned.1.call-update) | async-done | bytes 2359312 | tf_op jit(solution)/shard_map/all_gather | solution.py:212
  603.2 117.3 %while.28 = (s32[]{:T(128)}, f32[8,1024,72]{1,2,0:T(8,128)}, f32[8,1024,72]{1,2,0:T(8,128)}, bf16[2,8,512,72]{2,3,1,0:T(8,128)(2,1)}, bf16[2,8,512,72]{2,3,1,0:T...) while((s32[]{:T(128)}, f32[8,1024,72]{1,2,0:T(8,128)}, ...), condition=%wide.region_16.17_spmd.clone, body=%wide.region_14.16_spmd.clone.sunk | while | flops 3073470464 | bytes 271434112 | solution.py:257
  604.4 8.2 fusion.145
  612.6 10.3 select_add_fusion.5
  622.9 14.5 %multiply_reduce_fusion.10 = (f32[8,512]{1,0:T(8,128)S(1)}, f32[8,512,1024]{2,1,0:T(8,128)}) fusion(f32[8,512,1024]{2,1,0:T(8,128)} %fusion.145, f32[8,512]{1,0:T(8,128)S(1)} %dynamic-slice_bitcast_fusion.3, bf16[8,1024,72]{1,2,0:T(8,128)(2,1)} %copy-done.8, bf16[2,8,512,72]{2,3,1,0:T(8,128)(2,1)} %get-tuple-element.402, s32[]{:T(128)S(6)} %copy.93), kind=kOutput, calls=%fused_computation.15.clone.1 | convolution fusion | flops 620752896 | bytes 35356676 | tf_op jit(solution)/shard_map/while/body/eval_jaxpr/hqd,hkd->hqk/dot_general | solution.py:232
  639.7 10.5 multiply_convert_fusion.8
  669.7 11.1 select_add_fusion.5
  680.8 14.5 %multiply_reduce_fusion.10 = (f32[8,512]{1,0:T(8,128)S(1)}, f32[8,512,1024]{2,1,0:T(8,128)}) fusion(f32[8,512,1024]{2,1,0:T(8,128)} %fusion.145, f32[8,512]{1,0:T(8,128)S(1)} %dynamic-slice_bitcast_fusion.3, bf16[8,1024,72]{1,2,0:T(8,128)(2,1)} %copy-done.8, bf16[2,8,512,72]{2,3,1,0:T(8,128)(2,1)} %get-tuple-element.402, s32[]{:T(128)S(6)} %copy.93), kind=kOutput, calls=%fused_computation.15.clone.1 | convolution fusion | flops 620752896 | bytes 35356676 | tf_op jit(solution)/shard_map/while/body/eval_jaxpr/hqd,hkd->hqk/dot_general | solution.py:232
  697.6 10.5 multiply_convert_fusion.8
  738.7 12.4 fusion.75
  751.1 11.3 fusion.87
  762.7 9.5 fusion.42
  781.4 8.6 all-reduce.12
  807.6 61.9 %all-reduce.10 = (f32[6912]{0:T(1024)}, f32[2,1152]{1,0:T(2,128)}, f32[1152]{0:T(1024)}, f32[4608]{0:T(1024)}, f32[1152]{0:T(1024)}) all-reduce(bf16[6912]{0:T(1024)(128)(2,1)} %copy-done.41, bf16[2,1152]{1,0:T(2,128)(2,1)} %get-tuple-element.224, f32[1152]{0:T(1024)} %convert_reduce_fusion.2, ...), channel_id=7, replica_groups=mesh['fsdp'=16,'tp'=2] {'fsdp'}, use_global_device_ids=true, to_apply=%region_28.29.clone | all-reduce | flops 16128 | bytes 101376
  880.6 80.3 %reduce-scatter.27.cloned.1.call-done = f32[2304,72]{0,1:T(8,128)} async-done(((f32[2304,1152]{0,1:T(8,128)}), f32[2304,72]{0,1:T(8,128)}) %reduce-scatter.27.cloned.1.call-update) | async-done | bytes 663568 | tf_op jit(solution)/shard_map/reduce_scatter | solution.py:320
  960.8 124.5 %reduce-scatter.25.cloned.1.call-done = f32[72,2304]{1,0:T(8,128)} async-done(((f32[1152,2304]{1,0:T(8,128)}), f32[72,2304]{1,0:T(8,128)}) %reduce-scatter.25.cloned.1.call-update) | async-done | bytes 663568 | tf_op jit(solution)/shard_map/reduce_scatter | solution.py:318
  1085.3 111.3 %reduce-scatter.23.cloned.1.call-done = f32[72,3,576]{2,0,1:T(8,128)} async-done(((f32[1152,3,576]{2,0,1:T(8,128)}), f32[72,3,576]{2,0,1:T(8,128)}) %reduce-scatter.23.cloned.1.call-update) | async-done | bytes 497680 | tf_op jit(solution)/shard_map/reduce_scatter | solution.py:314
  1196.7 191.4 %reduce-scatter.21.cloned.1.call-done = f32[576,432]{0,1:T(8,128)} async-done(((f32[576,6912]{0,1:T(8,128)}), f32[576,432]{0,1:T(8,128)}) %reduce-scatter.21.cloned.1.call-update) | async-done | bytes 995344 | tf_op jit(solution)/shard_map/reduce_scatter | solution.py:312
  (354 shorter events, 319.7 us)
Async XLA Ops:
  7.2 84.4 %all-gather.10.cloned.1.call-start = ((), (), s32[]{:S(2)}) async-start(), calls=%async_computation.9 | async-start | bytes 9400320 | tf_op jit(solution)/shard_map/all_gather | solution.py:104
  7.9 135.8 %all-gather.14.cloned.1.call-start = ((), (), s32[]{:S(2)}) async-start(), calls=%async_computation.11 | async-start | bytes 4700160 | tf_op jit(solution)/shard_map/all_gather | solution.py:106
  8.7 171.8 %all-gather.12.cloned.1.call-start = ((), (), s32[]{:S(2)}) async-start(), calls=%async_computation.10 | async-start | bytes 3538944 | tf_op jit(solution)/shard_map/all_gather | solution.py:133
  108.6 113.3 %all-gather.16.cloned.1.call-start = ((), (), s32[]{:S(2)}) async-start(), calls=%async_computation.12 | async-start | bytes 1566720 | tf_op jit(solution)/shard_map/all_gather | solution.py:108
  109.2 208.7 %reduce-scatter.13.cloned.1.call-start = ((), (), s32[]{:S(2)}) async-start(), calls=%async_computation.13 | async-start | bytes 7077888 | tf_op jit(solution)/shard_map/reduce_scatter | solution.py:167
  228.0 120.0 %all-gather.20.cloned.1.call-start = ((), (), s32[]{:S(2)}) async-start(), calls=%async_computation.15 | async-start | bytes 5640192 | tf_op jit(solution)/shard_map/all_gather | solution.py:110
  228.1 9.5 collective-permute-start
  238.3 9.3 collective-permute-start.1
  238.3 9.4 collective-permute-start.8
  247.6 9.3 collective-permute-start.2
  247.7 9.3 collective-permute-start.9
  257.0 9.3 collective-permute-start.3
  257.0 9.3 collective-permute-start.10
  266.3 9.3 collective-permute-start.4
  267.1 9.2 collective-permute-start.11
  275.7 9.4 collective-permute-start.5
  276.4 9.8 collective-permute-start.12
  285.2 9.7 collective-permute-start.6
  285.2 99.6 %all-gather.18.cloned.1.call-start = ((), (), s32[]{:S(2)}) async-start(), calls=%async_computation.14 | async-start | bytes 3538944 | tf_op jit(solution)/shard_map/all_gather | solution.py:175
  286.1 10.7 collective-permute-start.13
  294.8 11.7 collective-permute-start.7
  296.8 35.7 %collective-permute-start.14 = (bf16[2304,72]{0,1:T(8,128)(2,1)}, bf16[2304,72]{0,1:T(8,128)(2,1)}, u32[]{:S(2)}, u32[]{:S(2)}) collective-permute-start(bf16[2304,72]{0,1:T(8,128)(2,1)} %collective-permute-done.13), channel_id=1, source_target_pairs={{2,0},{4,2},{6,4},{8,6},{10,8},{12,10},{14,12},{16,14},{18,16},{20... | collective-permute-start | bytes 995336 | tf_op jit(solution)/shard_map/ppermute | solution.py:27
  323.4 99.7 %all-gather.22.cloned.1.call-start = ((), (), s32[]{:S(2)}) async-start(), calls=%async_computation.17 | async-start | bytes 3538944 | tf_op jit(solution)/shard_map/all_gather | solution.py:194
  330.7 178.1 %reduce-scatter.17.cloned.1.call-start = ((), (), s32[]{:S(2)}) async-start(), calls=%async_computation.18 | async-start | bytes 7077888 | tf_op jit(solution)/shard_map/reduce_scatter | solution.py:203
  448.7 97.0 %reduce-scatter.15.cloned.1.call-start = ((), (), s32[]{:S(2)}) async-start(), calls=%async_computation.16 | async-start | bytes 3538944 | tf_op jit(solution)/shard_map/reduce_scatter | solution.py:185
  462.5 128.2 %all-gather.24.cloned.1.call-start = ((), (), s32[]{:S(2)}) async-start(), calls=%async_computation.19 | async-start | bytes 3538944 | tf_op jit(solution)/shard_map/all_gather | solution.py:212
  554.5 220.9 %reduce-scatter.19.cloned.1.call-start = ((), (), s32[]{:S(2)}) async-start(), calls=%async_computation.20 | async-start | bytes 3538944 | tf_op jit(solution)/shard_map/reduce_scatter | solution.py:268
  732.1 148.5 %reduce-scatter.29.cloned.1.call-start = ((), (), s32[]{:S(2)}) async-start(), calls=%async_computation.25 | async-start | bytes 3133440
  738.0 222.9 %reduce-scatter.27.cloned.1.call-start = ((), (), s32[]{:S(2)}) async-start(), calls=%async_computation.24 | async-start | bytes 11280384 | tf_op jit(solution)/shard_map/reduce_scatter | solution.py:320
  751.1 334.3 %reduce-scatter.25.cloned.1.call-start = ((), (), s32[]{:S(2)}) async-start(), calls=%async_computation.23 | async-start | bytes 11280384 | tf_op jit(solution)/shard_map/reduce_scatter | solution.py:318
  762.4 434.2 %reduce-scatter.23.cloned.1.call-start = ((), (), s32[]{:S(2)}) async-start(), calls=%async_computation.22 | async-start | bytes 9400320 | tf_op jit(solution)/shard_map/reduce_scatter | solution.py:314
  772.2 615.8 %reduce-scatter.21.cloned.1.call-start = ((), (), s32[]{:S(2)}) async-start(), calls=%async_computation.21 | async-start | bytes 18800640 | tf_op jit(solution)/shard_map/reduce_scatter | solution.py:312
  (79 other events, 899.0 us)
Sparse Core Ops, SparseCore 0:
  10.2 81.3 all-gather.9
  93.7 49.9 all-gather.13
  145.8 34.5 all-gather.11
  182.4 39.3 all-gather.15
  228.1 58.9 reduce-scatter.12
  289.4 58.5 all-gather.19
  350.2 34.6 all-gather.17
  387.0 36.0 all-gather.21
  448.8 59.9 reduce-scatter.16
  511.0 34.7 reduce-scatter.14
  554.6 36.0 all-gather.23
  732.2 34.6 reduce-scatter.18
  771.4 65.4 reduce-scatter.28
  841.4 119.4 reduce-scatter.26
  965.3 119.9 reduce-scatter.24
  1089.9 106.6 reduce-scatter.22
  1201.8 186.1 reduce-scatter.20
